TPU v7x, 32 devices: a whole 2x2x4 slice. The times are simulated.
32 devices in a mesh: batch: 16 (over z, y, x), stream: 2 (over core).
Axes of the slice: x: 2, y: 2, z: 4, core: 2. Of those that a mesh axis runs over, the one named last changes fastest.
Arguments:
- tokens: bfloat16 [128, 198, 768], P(('batch', 'stream')), may hold values from -6 to 6
- prompts: float32 [50, 768], replicated, may hold values from -6 to 6
- keep_mask: int32 [128, 196], P(('batch', 'stream')), may hold values from 0 to 1, as said below
- counts: int32 [128], P(('batch', 'stream')), may hold values from 79 to 196, as said below
- ln1_gain: float32 [768], replicated, may hold values from 0.5 to 1.5
- ln1_bias: float32 [768], replicated, may hold values from -0.6 to 0.6
- w_qkv: bfloat16 [768, 2304], replicated, may hold values from -0.21875 to 0.21875
- q_bias: float32 [768], replicated, may hold values from -0.6 to 0.6
- v_bias: float32 [768], replicated, may hold values from -0.6 to 0.6
- w_out: bfloat16 [768, 768], replicated, may hold values from -2.5 to 2.5
- out_bias: float32 [768], replicated, may hold values from -0.6 to 0.6
- ln2_gain: float32 [768], replicated, may hold values from 0.5 to 1.5
- ln2_bias: float32 [768], replicated, may hold values from -0.6 to 0.6
- w_fc1: bfloat16 [768, 3072], replicated, may hold values from -0.21875 to 0.21875
- fc1_bias: float32 [3072], replicated, may hold values from -0.6 to 0.6
- w_fc2: bfloat16 [3072, 768], replicated, may hold values from -0.109375 to 0.109375
- fc2_bias: float32 [768], replicated, may hold values from -0.6 to 0.6
- cot_seq: bfloat16 [128, 198, 768], P(('batch', 'stream')), may hold values from -6 to 6
- cot_prompt: bfloat16 [128, 50, 768], P(('batch', 'stream')), may hold values from -6 to 6
Outputs:
- layer_out: bfloat16 [128, 198, 768], P(('batch', 'stream'))
- prompt_out: bfloat16 [128, 50, 768], P(('batch', 'stream'))
- input_grad: float32 [128, 198, 768], P(('batch', 'stream'))
- prompt_grad: float32 [50, 768], replicated
- penalty: float32 [], replicated
Inputs may be any that keep to these rules, and one draw needn't show every extreme that they name: `keep_mask`: 1 keeps a patch; row i has exactly counts[i] ones. counts[i] is the number of ones in row i of keep_mask.
All inputs are finite; a program needn't handle non-finite values.
Results may differ from a plain program's by a relative error of at most 0.01.
Values sent between devices are 32-bit elements; how exact they have to be, the bound alone decides.
A program may use at most 128 MiB of HBM per device.

v0:
```python
import math
import jax
import jax.numpy as jnp
from jax import lax
from jax.sharding import PartitionSpec as P

HEADS = 12
EPSILON = 1e-06


def layer_norm(values_in, norm_gain, norm_shift):
    row_mean = jnp.mean(values_in, axis=-1, keepdims=True)
    centered = values_in - row_mean
    variance = jnp.mean(centered * centered, axis=-1, keepdims=True)
    return centered * lax.rsqrt(variance + EPSILON) * norm_gain + norm_shift


def split_heads(tensor, head_count):
    return tensor.reshape(
        tensor.shape[0], tensor.shape[1], head_count, tensor.shape[2] // head_count
    )


def masked_scores(queries, key_part, live_keys, head_count, score_scale):
    raw_scores = jnp.einsum(
        "iqhd,ikhd->ihqk",
        split_heads(queries, head_count),
        split_heads(key_part, head_count),
        preferred_element_type=jnp.float32,
    )
    return jnp.where(live_keys[:, None, None, :], raw_scores * score_scale, -1e30)


def project_pairs(pair_grads, pair_weight):
    return jnp.einsum("pe,de->pd", pair_grads, pair_weight, precision=lax.Precision.HIGHEST)


def body(
    tokens,
    prompts,
    keep_mask,
    counts,
    ln1_gain,
    ln1_bias,
    w_qkv,
    q_bias,
    v_bias,
    w_out,
    out_bias,
    ln2_gain,
    ln2_bias,
    w_fc1,
    fc1_bias,
    w_fc2,
    fc2_bias,
    cot_seq,
    cot_prompt,
):
    images, seq_length, model_width = tokens.shape
    prompt_count = prompts.shape[0]
    head_count = HEADS
    score_scale = (model_width // head_count) ** (-0.5)
    total_images = images * lax.axis_size("batch") * lax.axis_size("stream")
    count_sum = jnp.sum(counts.astype(jnp.float32))
    kept_total = lax.psum(count_sum, ("batch", "stream"))
    keep_full = jnp.concatenate(
        [jnp.ones((images, seq_length - keep_mask.shape[1]), jnp.int32), keep_mask], axis=1
    )
    kept_cols = keep_full[:, :, None] > 0
    live_keys = (
        jnp.concatenate([jnp.ones((images, prompt_count), jnp.int32), keep_full], axis=1) > 0
    )
    prompt_normed, prompt_norm_back = jax.vjp(
        lambda rows_in: layer_norm(rows_in, ln1_gain, ln1_bias), prompts
    )
    prompt_proj = jnp.dot(
        prompt_normed.astype(jnp.bfloat16), w_qkv, preferred_element_type=jnp.float32
    )
    prompt_query = (prompt_proj[:, :model_width] + q_bias).astype(jnp.bfloat16)
    prompt_pairs = jnp.concatenate(
        [prompt_proj[:, model_width : 2 * model_width], prompt_proj[:, 2 * model_width :] + v_bias],
        axis=1,
    ).astype(jnp.bfloat16)
    token_rows = tokens.astype(jnp.float32)
    token_normed, token_norm_back = jax.vjp(
        lambda rows_in: layer_norm(rows_in, ln1_gain, ln1_bias), token_rows
    )
    token_proj = jnp.einsum(
        "ihd,de->ihe", token_normed.astype(jnp.bfloat16), w_qkv, preferred_element_type=jnp.float32
    )
    token_query = (token_proj[..., :model_width] + q_bias).astype(jnp.bfloat16)
    token_pairs = jnp.concatenate(
        [
            token_proj[..., model_width : 2 * model_width],
            token_proj[..., 2 * model_width :] + v_bias,
        ],
        axis=2,
    ).astype(jnp.bfloat16)
    queries = jnp.concatenate(
        [jnp.broadcast_to(prompt_query[None], (images, prompt_count, model_width)), token_query],
        axis=1,
    )
    pairs = jnp.concatenate(
        [
            jnp.broadcast_to(prompt_pairs[None], (images, prompt_count, 2 * model_width)),
            token_pairs,
        ],
        axis=1,
    )
    key_part = pairs[..., :model_width]
    value_part = pairs[..., model_width:]
    value_heads = split_heads(value_part, head_count)
    scores = masked_scores(queries, key_part, live_keys, head_count, score_scale)
    top_score = jnp.max(scores, axis=-1, keepdims=True)
    log_total = top_score + jnp.log(jnp.sum(jnp.exp(scores - top_score), axis=-1, keepdims=True))
    soft_low = jnp.exp(scores - log_total).astype(jnp.bfloat16)
    context = jnp.einsum(
        "ihqk,ikhd->iqhd", soft_low, value_heads, preferred_element_type=jnp.float32
    )
    context = context.reshape(images, -1, model_width).astype(jnp.bfloat16)
    attention = (
        jnp.einsum("ird,de->ire", context, w_out, preferred_element_type=jnp.float32) + out_bias
    )
    residual = jnp.concatenate(
        [jnp.broadcast_to(prompts[None], (images, prompt_count, model_width)), token_rows], axis=1
    )
    middle = residual + attention
    second_norm, second_norm_back = jax.vjp(
        lambda rows_in: layer_norm(rows_in, ln2_gain, ln2_bias), middle
    )
    hidden = (
        jnp.einsum(
            "ird,df->irf",
            second_norm.astype(jnp.bfloat16),
            w_fc1,
            preferred_element_type=jnp.float32,
        )
        + fc1_bias
    )
    activated, gelu_back = jax.vjp(lambda rows_in: jax.nn.gelu(rows_in, approximate=False), hidden)
    result = (
        middle
        + jnp.einsum(
            "irf,fd->ird", activated.astype(jnp.bfloat16), w_fc2, preferred_element_type=jnp.float32
        )
        + fc2_bias
    )
    prompt_out = result[:, :prompt_count].astype(jnp.bfloat16)
    layer_out = jnp.where(kept_cols, result[:, prompt_count:], token_rows).astype(jnp.bfloat16)
    grad_result = jnp.concatenate(
        [cot_prompt, jnp.where(kept_cols, cot_seq, jnp.zeros_like(cot_seq))], axis=1
    )
    grad_act = jnp.einsum("ird,fd->irf", grad_result, w_fc2, preferred_element_type=jnp.float32)
    grad_hidden = gelu_back(grad_act)[0].astype(jnp.bfloat16)
    grad_second = jnp.einsum("irf,df->ird", grad_hidden, w_fc1, preferred_element_type=jnp.float32)
    grad_middle = grad_result.astype(jnp.float32) + second_norm_back(grad_second)[0]
    grad_context = jnp.einsum(
        "ire,de->ird", grad_middle.astype(jnp.bfloat16), w_out, preferred_element_type=jnp.float32
    ).astype(jnp.bfloat16)
    again = masked_scores(queries, key_part, live_keys, head_count, score_scale)
    soft_full = jnp.exp(again - log_total)
    soft_back = soft_full.astype(jnp.bfloat16)
    context_heads = split_heads(grad_context, head_count)
    grad_soft = jnp.einsum(
        "iqhd,ikhd->ihqk", context_heads, value_heads, preferred_element_type=jnp.float32
    )
    grad_values = jnp.einsum(
        "ihqk,iqhd->ikhd", soft_back, context_heads, preferred_element_type=jnp.float32
    ).reshape(images, -1, model_width)
    row_dot = jnp.sum(soft_full * grad_soft, axis=-1, keepdims=True)
    grad_scores = (soft_full * (grad_soft - row_dot)).astype(jnp.bfloat16)
    grad_queries = (
        jnp.einsum(
            "ihqk,ikhd->iqhd",
            grad_scores,
            split_heads(key_part, head_count),
            preferred_element_type=jnp.float32,
        )
        * score_scale
    )
    grad_queries = grad_queries.reshape(images, -1, model_width).astype(jnp.bfloat16)
    grad_keys = (
        jnp.einsum(
            "ihqk,iqhd->ikhd",
            grad_scores,
            split_heads(queries, head_count),
            preferred_element_type=jnp.float32,
        )
        * score_scale
    ).reshape(images, -1, model_width)
    grad_pairs = jnp.concatenate([grad_keys, grad_values], axis=2)
    token_proj_grad = jnp.concatenate(
        [grad_queries[:, prompt_count:], grad_pairs[:, prompt_count:].astype(jnp.bfloat16)], axis=2
    )
    grad_token_normed = jnp.einsum(
        "ihe,de->ihd", token_proj_grad, w_qkv, preferred_element_type=jnp.float32
    )
    grad_tokens = grad_middle[:, prompt_count:] + token_norm_back(grad_token_normed)[0]
    input_grad = jnp.where(kept_cols, grad_tokens, cot_seq.astype(jnp.float32))
    pair_weight = w_qkv[:, model_width:].astype(jnp.float32)
    pair_local = jnp.sum(grad_pairs[:, :prompt_count], axis=0)
    query_normed = jnp.sum(
        jnp.einsum(
            "ipe,de->ipd",
            grad_queries[:, :prompt_count],
            w_qkv[:, :model_width],
            preferred_element_type=jnp.float32,
        ),
        axis=0,
    )
    middle_sum = jnp.sum(grad_middle[:, :prompt_count], axis=0)
    prompt_local = prompt_norm_back(query_normed)[0] + middle_sum
    pair_total = lax.psum(pair_local, ("batch", "stream"))
    prompt_total = lax.psum(prompt_local, ("batch", "stream"))
    prompt_total = prompt_total + prompt_norm_back(project_pairs(pair_total, pair_weight))[0]
    penalty_weight = kept_total / (keep_mask.shape[1] * math.sqrt(total_images))
    prompt_grad = prompt_total + 2.0 * penalty_weight * prompts
    penalty = penalty_weight * jnp.sum(prompts * prompts) / (prompt_count * model_width)
    return (layer_out, prompt_out, input_grad, prompt_grad, penalty)


def solution(mesh):
    in_specs = (
        P(("batch", "stream"), None, None),
        P(),
        P(("batch", "stream"), None),
        P(("batch", "stream")),
        P(),
        P(),
        P(),
        P(),
        P(),
        P(),
        P(),
        P(),
        P(),
        P(),
        P(),
        P(),
        P(),
        P(("batch", "stream"), None, None),
        P(("batch", "stream"), None, None),
    )
    out_specs = (
        P(("batch", "stream"), None, None),
        P(("batch", "stream"), None, None),
        P(("batch", "stream"), None, None),
        P(),
        P(),
    )
    return jax.shard_map(body, mesh=mesh, in_specs=in_specs, out_specs=out_specs, check_vma=False)
```

profile of v0, /device:TPU:10, one launch (start us, length us, event | category | flops | bytes accessed | tf_op | source)
XLA Modules:
  0.0 464.4 jit_solution(8597299555711745016)
XLA Ops:
  10.7 5.8 %fusion.29 = f32[4,198,2304]{2,1,0:T(8,128)S(1)} fusion(bf16[768,2304]{1,0:T(8,128)(2,1)} %param.25, f32[768]{0:T(1024)} %param.24, f32[768]{0:T(1024)} %param.23, f32[4,198]{1,0:T(4,128)S(1)} %fusion.73, f32[4,198]{1,0:T(4,128)S(1)} %broadcast_multiply_fusion.1, bf16[4,198,768]{2,0,1:T(4,128)(2,1)} %param.19), kind=kOutput, calls=%fused_computation.49 | convolution fusion | flops 2806493184 | bytes 12067008 | tf_op jit(solution)/shard_map/ihd,de->ihe/dot_general | solution.py:88
  16.5 3.0 copy-done.17
  21.0 2.8 fusion.68
  23.8 4.0 fusion.35
  32.1 2.7 copy.49
  35.0 2.7 pad_maximum_fusion
  37.7 2.6 copy.50
  40.3 2.6 copy.51
  42.9 5.0 %fusion.6 = (f32[4,12,248]{2,1,0:T(8,128)S(1)}, f32[4,12,248,248]{2,3,1,0:T(8,128)S(1)}) fusion(pred[4,248]{1,0:T(4,128)(4,1)S(1)} %add_compare_fusion, bf16[4,248,12,64]{1,3,2,0:T(8,128)(2,1)} %bitcast.72, bf16[4,248,12,64]{1,3,2,0:T(8,128)(2,1)} %bitcast.70), kind=kOutput, calls=%fused_computation.26 | convolution fusion | flops 386725248 | bytes 14904800 | tf_op jit(solution)/shard_map/iqhd,ikhd->ihqk/dot_general | solution.py:25
  47.9 3.4 exponential_reduce_fusion
  52.5 3.1 convolution_convert_fusion
  58.8 13.1 %fusion.32 = (u8[248,3072]{1,0:T(8,128)(4,1)S(1)}, u8[248,3072]{1,0:T(8,128)(4,1)S(1)}, f32[4,248,3072]{2,1,0:T(8,128)}) fusion(f32[3072]{0:T(1024)S(1)} %copy-done.29, bf16[768,3072]{1,0:T(8,128)(2,1)S(1)} %bitcast.83, f32[4,248,768]{2,1,0:T(8,128)S(1)} %get-tuple-element.36, f32[768]{0:T(1024)S(1)} %copy-done.34, f32[768]{0:T(1024)S(1)} %copy-done.25, ...), kind=kOutput, calls=%fused_computation.60 | convolution fusion | flops 4725792768 | bytes 21505792 | tf_op jit(solution)/shard_map/ird,df->irf/dot_general | solution.py:132
  71.9 29.0 %fusion = f32[4,248,3072]{2,1,0:T(8,128)} fusion(f32[4,248,3072]{2,1,0:T(8,128)} %get-tuple-element.37, f32[3072]{0:T(1024)S(1)} %copy-done.29, u8[248,3072]{1,0:T(8,128)(4,1)S(1)} %get-tuple-element.16, u8[248,3072]{1,0:T(8,128)(4,1)S(1)} %get-tuple-element.15), kind=kLoop, calls=%fused_computation.1 | loop fusion | flops 207224832 | bytes 25915392 | tf_op jit(solution)/shard_map/jvp()/erfc | solution.py:140
  100.9 14.7 %add_add_fusion.3 = bf16[4,248,768]{2,1,0:T(8,128)(2,1)S(1)} fusion(f32[4,248,768]{2,1,0:T(8,128)S(1)} %get-tuple-element.36, bf16[3072,768]{1,0:T(8,128)(2,1)} %param.34, f32[4,248,3072]{2,1,0:T(8,128)} %fusion, f32[4,248,3072]{2,1,0:T(8,128)} %get-tuple-element.37, f32[3072]{0:T(1024)S(1)} %copy-done.29, f32[768]{0:T(1024)S(1)} %copy-done.35), kind=kOutput, calls=%fused_computation.56 | convolution fusion | flops 4695318528 | bytes 33684480 | tf_op jit(solution)/shard_map/irf,fd->ird/dot_general | solution.py:143
  117.9 19.5 %multiply_reduce_fusion.1 = (f32[4,248]{1,0:T(4,128)S(1)}, f32[4,248,768]{2,1,0:T(8,128)}) fusion(f32[4,248,768]{2,1,0:T(8,128)} %copy-done.4, f32[768]{0:T(1024)S(1)} %copy-done.25, f32[4,248]{1,0:T(4,128)S(1)} %broadcast_multiply_fusion, bf16[768,3072]{1,0:T(8,128)(2,1)} %param.32, f32[4,248,3072]{2,1,0:T(8,128)} %fusion, ...), kind=kOutput, calls=%fused_computation.55 | convolution fusion | flops 9413491712 | bytes 41458432 | tf_op jit(solution)/shard_map/irf,df->ird/dot_general | solution.py:155
  137.5 3.5 fusion.60
  146.2 2.6 convolution_convert_fusion.1
  148.8 2.6 copy.56
  151.5 14.3 %multiply_reduce_fusion = (f32[4,12,248]{2,1,0:T(8,128)S(1)}, f32[4,12,248,248]{2,3,1,0:T(8,128)}) fusion(f32[4,12,248,248]{2,3,1,0:T(8,128)} %copy-done.1, f32[4,12,248]{2,1,0:T(8,128)S(1)} %log_add_fusion, pred[4,248]{1,0:T(4,128)(4,1)S(1)} %add_compare_fusion, bf16[4,248,12,64]{1,3,2,0:T(8,128)(2,1)} %bitcast.74, bf16[4,248,12,64]{1,3,2,0:T(8,128)(2,1)} %bitcast.80), kind=kOutput, calls=%fused_computation.8 | convolution fusion | flops 392629632 | bytes 26761184 | tf_op jit(solution)/shard_map/iqhd,ikhd->ihqk/dot_general | solution.py:164
  165.8 9.0 %fusion.64 = f32[4,12,64,248]{3,2,1,0:T(8,128)} fusion(bf16[4,248,12,64]{1,3,2,0:T(8,128)(2,1)S(1)} %bitcast.75, f32[4,12,248,248]{2,3,1,0:T(8,128)} %copy-done.1, f32[4,12,248]{2,1,0:T(8,128)S(1)} %log_add_fusion, pred[4,248]{1,0:T(4,128)(4,1)S(1)} %add_compare_fusion), kind=kOutput, calls=%fused_computation.121 | convolution fusion | flops 389689344 | bytes 16428512 | tf_op jit(solution)/shard_map/ihqk,iqhd->ikhd/dot_general | solution.py:167
  174.8 6.9 %multiply_convert_fusion = bf16[4,12,248,248]{2,3,1,0:T(8,128)(2,1)S(1)} fusion(f32[4,12,248,248]{2,3,1,0:T(8,128)} %get-tuple-element.41, f32[4,12,248,248]{2,3,1,0:T(8,128)S(1)} %bitcast.69, f32[4,12,248]{2,1,0:T(8,128)S(1)} %get-tuple-element.40, f32[4,12,248]{2,1,0:T(8,128)S(1)} %log_add_fusion, pred[4,248]{1,0:T(4,128)(4,1)S(1)} %add_compare_fusion), kind=kLoop, calls=%fused_computation.7 | loop fusion | flops 17713152 | bytes 29618144 | tf_op jit(solution)/shard_map/convert_element_type | solution.py:171
  181.8 3.7 convolution_multiply_fusion
  185.5 3.5 copy.61
  189.0 3.6 copy.62
  195.1 4.5 fusion.13
  199.6 4.0 multiply_convert_fusion.3
  209.0 6.3 %multiply_reduce_fusion.3 = (f32[4,198]{1,0:T(4,128)S(1)}, f32[4,198,768]{2,1,0:T(8,128)S(1)}) fusion(f32[768]{0:T(1024)S(1)} %copy-done.24, f32[4,198]{1,0:T(4,128)S(1)} %broadcast_multiply_fusion.1, bf16[4,198,768]{2,0,1:T(4,128)(2,1)S(1)} %copy-done.3, bf16[768,2304]{1,0:T(8,128)(2,1)} %param.25, bf16[4,198,1536]{2,1,0:T(8,128)(2,1)} %fusion.13, ...), kind=kOutput, calls=%fused_computation.70 | convolution fusion | flops 2813183232 | bytes 10847424 | tf_op jit(solution)/shard_map/ihe,de->ihd/dot_general | solution.py:195
  222.3 41.6 %psum.23 = f32[]{:T(128)} all-reduce(f32[]{:T(128)} %convert_reduce_fusion.1), channel_id=1, replica_groups=mesh['batch'=16,'stream'=2] {'batch','stream'}, use_global_device_ids=true, to_apply=%region_23.24 | all-reduce | flops 1 | bytes 8 | tf_op jit(solution)/shard_map/psum | solution.py:65
  263.9 2.9 copy.65
  272.5 51.0 %all-reduce.6.cloned.1.call-done = f32[50,1536]{1,0:T(8,128)} async-done(((f32[50,1536]{1,0:T(8,128)}), f32[50,1536]{1,0:T(8,128)}) %all-reduce.6.cloned.1.call-update) | async-done | bytes 307216 | tf_op jit(solution)/shard_map/psum | solution.py:213
  323.6 4.6 multiply_reduce_fusion.5
  330.0 124.4 %all-reduce.4.cloned.1.call-done = f32[50,768]{1,0:T(8,128)} async-done(((f32[50,768]{1,0:T(8,128)}), f32[50,768]{1,0:T(8,128)}) %all-reduce.4.cloned.1.call-update) | async-done | bytes 153616 | tf_op jit(solution)/shard_map/psum | solution.py:214
  (144 shorter events, 43.4 us)
Async XLA Ops:
  7.2 48.5 %copy-start = (bf16[768,768]{1,0:T(8,128)(2,1)S(1)}, bf16[768,768]{1,0:T(8,128)(2,1)}, u32[]{:S(2)}) copy-start(bf16[768,768]{1,0:T(8,128)(2,1)} %param.28) | copy-start | bytes 3538948
  7.2 316.4 %all-reduce.6.cloned.1.call-start = ((), (), s32[]{:S(2)}) async-start(), calls=%async_computation.1 | async-start | bytes 688128 | tf_op jit(solution)/shard_map/psum | solution.py:213
  10.6 10.0 %copy-start.12 = (f32[50,768]{1,0:T(8,128)S(1)}, f32[50,768]{1,0:T(8,128)}, u32[]{:S(2)}) copy-start(f32[50,768]{1,0:T(8,128)} %param.20) | copy-start | bytes 460804
  10.6 10.3 %copy-start.24 = (f32[768]{0:T(1024)S(1)}, f32[768]{0:T(1024)}, u32[]{:S(2)}) copy-start(f32[768]{0:T(1024)} %param.23) | copy-start | bytes 9220
  10.7 10.3 %copy-start.30 = (f32[768]{0:T(1024)S(1)}, f32[768]{0:T(1024)}, u32[]{:S(2)}) copy-start(f32[768]{0:T(1024)} %param.24) | copy-start | bytes 9220
  19.5 4.3 copy-start.26
  19.5 4.3 copy-start.27
  23.8 4.1 copy-start.3
  47.9 4.6 copy-start.1
  47.9 4.6 copy-start.16
  52.5 3.2 copy-start.21
  52.5 3.2 copy-start.33
  55.6 3.1 slice-start.4
  55.7 3.0 slice-start.5
  57.5 43.4 %copy-start.4 = (f32[4,248,768]{2,1,0:T(8,128)}, f32[4,248,768]{2,1,0:T(8,128)S(1)}, u32[]{:S(2)}) copy-start(f32[4,248,768]{2,1,0:T(8,128)S(1)} %get-tuple-element.36) | copy-start | bytes 9142276
  71.9 29.0 %copy-start.35 = (f32[768]{0:T(1024)S(1)}, f32[768]{0:T(1024)}, u32[]{:S(2)}) copy-start(f32[768]{0:T(1024)} %param.35) | copy-start | bytes 9220
  100.9 14.7 %copy-start.19 = (bf16[4,198,768]{2,0,1:T(4,128)(2,1)S(1)}, bf16[4,198,768]{2,0,1:T(4,128)(2,1)}, u32[]{:S(2)}) copy-start(bf16[4,198,768]{2,0,1:T(4,128)(2,1)} %param.36) | copy-start | bytes 3649540
  137.5 3.7 copy-start.5
  137.5 4.6 copy-start.11
  151.5 14.4 %copy-start.8 = (bf16[4,248,768]{1,2,0:T(8,128)(2,1)S(1)}, bf16[4,248,768]{1,2,0:T(8,128)(2,1)}, u32[]{:S(2)}) copy-start(bf16[4,248,768]{1,2,0:T(8,128)(2,1)} %copy.56) | copy-start | bytes 4571140
  151.5 23.4 %slice-start = ((s8[12189696]{0:T(1024)(128)(4,1)}), s8[4194304]{0:T(1024)(128)(4,1)S(1)}, s32[]{:S(2)}) async-start(s8[12189696]{0:T(1024)(128)(4,1)} %bitcast.68), calls=%async_computation.2 | async-start | bytes 8388608
  151.5 23.4 %slice-start.1 = ((s8[12189696]{0:T(1024)(128)(4,1)}), s8[3801088]{0:T(1024)(128)(4,1)S(1)}, s32[]{:S(2)}) async-start(s8[12189696]{0:T(1024)(128)(4,1)} %bitcast.68), calls=%async_computation.3 | async-start | bytes 7602176
  165.8 9.0 %slice-start.2 = ((s8[12189696]{0:T(1024)(128)(4,1)}), s8[4194304]{0:T(1024)(128)(4,1)S(1)}, s32[]{:S(2)}) async-start(s8[12189696]{0:T(1024)(128)(4,1)} %bitcast.68), calls=%async_computation.4 | async-start | bytes 8388608
  174.8 7.0 %copy-start.7 = (bf16[4,248,768]{1,2,0:T(8,128)(2,1)S(1)}, bf16[4,248,768]{1,2,0:T(8,128)(2,1)}, u32[]{:S(2)}) copy-start(bf16[4,248,768]{1,2,0:T(8,128)(2,1)} %copy.50) | copy-start | bytes 4571140
  181.8 3.7 copy-start.2
  194.8 259.7 %all-reduce.4.cloned.1.call-start = ((), (), s32[]{:S(2)}) async-start(), calls=%async_computation | async-start | bytes 344064 | tf_op jit(solution)/shard_map/psum | solution.py:214
  195.1 4.6 copy-start.6
  209.0 7.3 %copy-start.20 = (bf16[4,198,768]{2,0,1:T(4,128)(2,1)S(1)}, bf16[4,198,768]{2,0,1:T(4,128)(2,1)}, u32[]{:S(2)}) copy-start(bf16[4,198,768]{2,0,1:T(4,128)(2,1)} %param.36) | copy-start | bytes 3649540
  217.2 3.0 copy-start.15
  220.2 46.6 %slice-start.3 = ((bf16[4,248,768]{2,1,0:T(8,128)(2,1)}), bf16[4,50,768]{2,1,0:T(8,128)(2,1)S(1)}, s32[]{:S(2)}) async-start(bf16[4,248,768]{2,1,0:T(8,128)(2,1)} %copy-done.22), calls=%async_computation.5 | async-start | bytes 688128 | tf_op jit(solution)/shard_map/slice | solution.py:148
  263.9 3.8 copy-start.13
  270.1 58.1 %copy-start.32 = (f32[50]{0:T(128)S(1)}, f32[50]{0:T(128)}, u32[]{:S(2)}) copy-start(f32[50]{0:T(128)} %copy-done.31) | copy-start | bytes 604
  (13 other events, 23.8 us)
Sparse Core Ops, SparseCore 0:
  194.9 128.5 all-reduce.5
  330.6 123.8 all-reduce.3
where the time goes:
time: 470 us; the launch traced here: 464 us
  waiting for transfers between devices  175 us (37%)
  matrix products  112 us (24%)
  other arithmetic  75.7 us (16%)
  blocking collectives  41.6 us (9%)
  local copies, waits for them, and re-layouts  41.1 us (9%)
  between operations  17.9 us (4%)
    psum x1, waiting for transfers between devices, body(): prompt_total = lax.psum(prompt_local, ('batch', 'stream'))  124 us
    psum x1, waiting for transfers between devices, body(): pair_total = lax.psum(pair_local, ('batch', 'stream'))  51 us
    psum x1, blocking collectives, body(): kept_total = lax.psum(count_sum, ('batch', 'stream'))  41.6 us
    another operation x1, other arithmetic, body(): jax.nn.gelu(rows_in, approximate=False)  29 us
    dot_general x1, matrix products, body(): jnp.einsum('irf,df->ird', grad_hidden, w_fc1, preferred_element_type=jnp....  19.5 us
    unnamed x89, local copies, waits for them, and re-layouts  18.5 us
    dot_general x1, matrix products, body(): jnp.einsum('irf,fd->ird', activated.astype(jnp.bfloat16), w_fc2, preferre...  14.7 us
    dot_general x1, matrix products, body(): jnp.einsum('iqhd,ikhd->ihqk', context_heads, value_heads, preferred_eleme...  14.3 us
  transfers between devices with their start and end apart: 2, of which 2 were waited for; matrix products, arithmetic and copies ran while one was open for 7% of the time, Pallas kernels for 0%

commit v1 on v0

--- a/solution.py
+++ b/solution.py
@@ -211,7 +211,7 @@
     middle_sum = jnp.sum(grad_middle[:, :prompt_count], axis=0)
     prompt_local = prompt_norm_back(query_normed)[0] + middle_sum
     pair_total = lax.psum(pair_local, ("batch", "stream"))
-    prompt_total = lax.psum(prompt_local, ("batch", "stream"))
+    prompt_total = lax.all_gather(prompt_local, axis_name=("batch", "stream")).sum(axis=0)
     prompt_total = prompt_total + prompt_norm_back(project_pairs(pair_total, pair_weight))[0]
     penalty_weight = kept_total / (keep_mask.shape[1] * math.sqrt(total_images))
     prompt_grad = prompt_total + 2.0 * penalty_weight * prompts

time: 470 us -> 413 us (0.88)
  waiting for transfers between devices: 175 us -> 122 us
    psum x1 -> x0, waiting for transfers between devices: 124 us -> none  [body(): prompt_total = lax.psum(prompt_local, ('batch', 'stream'))]
    psum x1, waiting for transfers between devices: 51 us -> 120 us  [body(): pair_total = lax.psum(pair_local, ('batch', 'stream'))]
where the time goes in v1:
time: 413 us; the launch traced here: 407 us
  waiting for transfers between devices  122 us (30%)
  matrix products  110 us (27%)
  other arithmetic  75.2 us (18%)
  local copies, waits for them, and re-layouts  42.1 us (10%)
  blocking collectives  39.6 us (10%)
  between operations  17.7 us (4%)
    psum x1, waiting for transfers between devices, body(): pair_total = lax.psum(pair_local, ('batch', 'stream'))  120 us
    psum x1, blocking collectives, body(): kept_total = lax.psum(count_sum, ('batch', 'stream'))  39.6 us
    another operation x1, other arithmetic, body(): jax.nn.gelu(rows_in, approximate=False)  29 us
    dot_general x1, matrix products, body(): jnp.einsum('irf,df->ird', grad_hidden, w_fc1, preferred_element_type=jnp....  19.5 us
    unnamed x89, local copies, waits for them, and re-layouts  17.9 us
    dot_general x1, matrix products, body(): jnp.einsum('irf,fd->ird', activated.astype(jnp.bfloat16), w_fc2, preferre...  14.7 us
    dot_general x1, matrix products, body(): jnp.einsum('iqhd,ikhd->ihqk', context_heads, value_heads, preferred_eleme...  14.4 us
    dot_general x1, matrix products, body(): jnp.einsum('ird,df->irf', second_norm.astype(jnp.bfloat16), w_fc1, prefer...  13.1 us
  transfers between devices with their start and end apart: 2, of which 2 were waited for; matrix products, arithmetic and copies ran while one was open for 7% of the time, Pallas kernels for 0%

profile of v1, /device:TPU:10, one launch (start us, length us, event | category | flops | bytes accessed | tf_op | source)
XLA Modules:
  0.0 407.0 jit_solution(8998295568785090678)
XLA Ops:
  10.7 5.8 %fusion.29 = f32[4,198,2304]{2,1,0:T(8,128)S(1)} fusion(bf16[768,2304]{1,0:T(8,128)(2,1)} %param.25, f32[768]{0:T(1024)} %param.24, f32[768]{0:T(1024)} %param.23, f32[4,198]{1,0:T(4,128)S(1)} %fusion.73, f32[4,198]{1,0:T(4,128)S(1)} %broadcast_multiply_fusion.1, bf16[4,198,768]{2,0,1:T(4,128)(2,1)} %param.19), kind=kOutput, calls=%fused_computation.49 | convolution fusion | flops 2806493184 | bytes 12067008 | tf_op jit(solution)/shard_map/ihd,de->ihe/dot_general | solution.py:88
  16.5 3.0 copy-done.15
  21.0 2.8 fusion.68
  23.8 4.0 fusion.35
  32.1 2.7 copy.69
  35.1 2.7 pad_maximum_fusion
  40.3 2.6 copy.71
  42.9 5.0 %fusion.6 = (f32[4,12,248]{2,1,0:T(8,128)S(1)}, f32[4,12,248,248]{2,3,1,0:T(8,128)S(1)}) fusion(pred[4,248]{1,0:T(4,128)(4,1)S(1)} %add_compare_fusion, bf16[4,248,12,64]{1,3,2,0:T(8,128)(2,1)} %bitcast.74, bf16[4,248,12,64]{1,3,2,0:T(8,128)(2,1)} %bitcast.72), kind=kOutput, calls=%fused_computation.26 | convolution fusion | flops 386725248 | bytes 14904800 | tf_op jit(solution)/shard_map/iqhd,ikhd->ihqk/dot_general | solution.py:25
  48.0 3.4 exponential_reduce_fusion
  52.5 3.1 convolution_convert_fusion
  58.9 13.1 %fusion.32 = (u8[248,3072]{1,0:T(8,128)(4,1)S(1)}, u8[248,3072]{1,0:T(8,128)(4,1)S(1)}, f32[4,248,3072]{2,1,0:T(8,128)}) fusion(f32[3072]{0:T(1024)S(1)} %copy-done.31, bf16[768,3072]{1,0:T(8,128)(2,1)S(1)} %bitcast.85, f32[4,248,768]{2,1,0:T(8,128)S(1)} %get-tuple-element.41, f32[768]{0:T(1024)S(1)} %copy-done.34, f32[768]{0:T(1024)S(1)} %copy-done.27, ...), kind=kOutput, calls=%fused_computation.60 | convolution fusion | flops 4725792768 | bytes 21505792 | tf_op jit(solution)/shard_map/ird,df->irf/dot_general | solution.py:132
  71.9 29.0 %fusion = f32[4,248,3072]{2,1,0:T(8,128)} fusion(f32[4,248,3072]{2,1,0:T(8,128)} %get-tuple-element.42, f32[3072]{0:T(1024)S(1)} %copy-done.31, u8[248,3072]{1,0:T(8,128)(4,1)S(1)} %get-tuple-element.21, u8[248,3072]{1,0:T(8,128)(4,1)S(1)} %get-tuple-element.20), kind=kLoop, calls=%fused_computation.1 | loop fusion | flops 207224832 | bytes 25915392 | tf_op jit(solution)/shard_map/jvp()/erfc | solution.py:140
  101.0 14.7 %add_add_fusion.3 = bf16[4,248,768]{2,1,0:T(8,128)(2,1)S(1)} fusion(f32[4,248,768]{2,1,0:T(8,128)S(1)} %get-tuple-element.41, bf16[3072,768]{1,0:T(8,128)(2,1)} %param.34, f32[4,248,3072]{2,1,0:T(8,128)} %fusion, f32[4,248,3072]{2,1,0:T(8,128)} %get-tuple-element.42, f32[3072]{0:T(1024)S(1)} %copy-done.31, f32[768]{0:T(1024)S(1)} %copy-done.35), kind=kOutput, calls=%fused_computation.56 | convolution fusion | flops 4695318528 | bytes 33684480 | tf_op jit(solution)/shard_map/irf,fd->ird/dot_general | solution.py:143
  117.9 19.5 %multiply_reduce_fusion.1 = (f32[4,248]{1,0:T(4,128)S(1)}, f32[4,248,768]{2,1,0:T(8,128)}) fusion(f32[4,248,768]{2,1,0:T(8,128)} %copy-done.4, f32[768]{0:T(1024)S(1)} %copy-done.27, f32[4,248]{1,0:T(4,128)S(1)} %broadcast_multiply_fusion, bf16[768,3072]{1,0:T(8,128)(2,1)} %param.32, f32[4,248,3072]{2,1,0:T(8,128)} %fusion, ...), kind=kOutput, calls=%fused_computation.55 | convolution fusion | flops 9413491712 | bytes 41458432 | tf_op jit(solution)/shard_map/irf,df->ird/dot_general | solution.py:155
  137.5 3.5 fusion.60
  146.2 2.6 convolution_convert_fusion.1
  148.8 2.6 copy.76
  151.5 14.4 %multiply_reduce_fusion = (f32[4,12,248]{2,1,0:T(8,128)S(1)}, f32[4,12,248,248]{2,3,1,0:T(8,128)}) fusion(f32[4,12,248,248]{2,3,1,0:T(8,128)} %copy-done.1, f32[4,12,248]{2,1,0:T(8,128)S(1)} %log_add_fusion, pred[4,248]{1,0:T(4,128)(4,1)S(1)} %add_compare_fusion, bf16[4,248,12,64]{1,3,2,0:T(8,128)(2,1)} %bitcast.76, bf16[4,248,12,64]{1,3,2,0:T(8,128)(2,1)} %bitcast.82), kind=kOutput, calls=%fused_computation.8 | convolution fusion | flops 392629632 | bytes 26761184 | tf_op jit(solution)/shard_map/iqhd,ikhd->ihqk/dot_general | solution.py:164
  165.8 9.0 %fusion.64 = f32[4,12,64,248]{3,2,1,0:T(8,128)} fusion(bf16[4,248,12,64]{1,3,2,0:T(8,128)(2,1)S(1)} %bitcast.77, f32[4,12,248,248]{2,3,1,0:T(8,128)} %copy-done.1, f32[4,12,248]{2,1,0:T(8,128)S(1)} %log_add_fusion, pred[4,248]{1,0:T(4,128)(4,1)S(1)} %add_compare_fusion), kind=kOutput, calls=%fused_computation.121 | convolution fusion | flops 389689344 | bytes 16428512 | tf_op jit(solution)/shard_map/ihqk,iqhd->ikhd/dot_general | solution.py:167
  174.9 6.9 %multiply_convert_fusion = bf16[4,12,248,248]{2,3,1,0:T(8,128)(2,1)S(1)} fusion(f32[4,12,248,248]{2,3,1,0:T(8,128)} %get-tuple-element.46, f32[4,12,248,248]{2,3,1,0:T(8,128)S(1)} %bitcast.71, f32[4,12,248]{2,1,0:T(8,128)S(1)} %get-tuple-element.45, f32[4,12,248]{2,1,0:T(8,128)S(1)} %log_add_fusion, pred[4,248]{1,0:T(4,128)(4,1)S(1)} %add_compare_fusion), kind=kLoop, calls=%fused_computation.7 | loop fusion | flops 17713152 | bytes 29618144 | tf_op jit(solution)/shard_map/convert_element_type | solution.py:171
  181.8 3.7 convolution_multiply_fusion
  185.5 3.5 copy.81
  189.0 3.6 copy.82
  195.1 4.4 %multiply_convert_fusion.3 = bf16[4,12,64,248]{3,2,1,0:T(8,128)(2,1)S(1)} fusion(bf16[4,248,12,64]{1,3,2,0:T(8,128)(2,1)} %bitcast.73, bf16[4,12,248,248]{2,3,1,0:T(8,128)(2,1)} %copy-done.2), kind=kOutput, calls=%fused_computation.51 | convolution fusion | flops 379404288 | bytes 8951808 | tf_op jit(solution)/shard_map/ihqk,ikhd->iqhd/dot_general | solution.py:173
  203.9 119.7 %all-reduce.3.cloned.1.call-done = f32[50,1536]{1,0:T(8,128)} async-done(((f32[50,1536]{1,0:T(8,128)}), f32[50,1536]{1,0:T(8,128)}) %all-reduce.3.cloned.1.call-update) | async-done | bytes 307216 | tf_op jit(solution)/shard_map/psum | solution.py:213
  323.6 4.6 %multiply_reduce_fusion.5 = (f32[]{:T(128)}, f32[50]{0:T(128)S(1)}, f32[50,768]{1,0:T(8,128)S(1)}) fusion(f32[50,768]{1,0:T(8,128)S(1)} %copy-done.11, f32[50]{0:T(128)S(1)} %broadcast_multiply_fusion.2, f32[768]{0:T(1024)S(1)} %copy-done.24, f32[50,1536]{1,0:T(8,128)} %all-reduce.3.cloned.1.call-done, bf16[768,2304]{1,0:T(8,128)(2,1)} %param.25), kind=kOutput, calls=%fused_computation.114 | convolution fusion | flops 708019136 | bytes 3014036 | tf_op jit(solution)/shard_map/pe,de->pd/dot_general | solution.py:35
  330.0 39.6 %psum.15 = f32[]{:T(128)} all-reduce(f32[]{:T(128)} %convert_reduce_fusion.1), channel_id=1, replica_groups=mesh['batch'=16,'stream'=2] {'batch','stream'}, use_global_device_ids=true, to_apply=%region_23.24 | all-reduce | flops 1 | bytes 8 | tf_op jit(solution)/shard_map/psum | solution.py:65
  369.6 3.5 slice.87
  377.9 3.1 fusion.13
  381.8 3.3 multiply_reduce_fusion.3
  392.5 2.7 all-gather.4.cloned.1.call-done
  395.2 2.8 reduce_sum.246
  (145 shorter events, 44.4 us)
Async XLA Ops:
  7.2 48.6 %copy-start = (bf16[768,768]{1,0:T(8,128)(2,1)S(1)}, bf16[768,768]{1,0:T(8,128)(2,1)}, u32[]{:S(2)}) copy-start(bf16[768,768]{1,0:T(8,128)(2,1)} %param.28) | copy-start | bytes 3538948
  7.2 316.4 %all-reduce.3.cloned.1.call-start = ((), (), s32[]{:S(2)}) async-start(), calls=%async_computation | async-start | bytes 688128 | tf_op jit(solution)/shard_map/psum | solution.py:213
  10.6 5.9 %copy-start.25 = (f32[4,198]{1,0:T(4,128)}, f32[4,198]{1,0:T(4,128)S(1)}, u32[]{:S(2)}) copy-start(f32[4,198]{1,0:T(4,128)S(1)} %multiply_reduce_fusion.4) | copy-start | bytes 9508
  10.6 10.0 %copy-start.11 = (f32[50,768]{1,0:T(8,128)S(1)}, f32[50,768]{1,0:T(8,128)}, u32[]{:S(2)}) copy-start(f32[50,768]{1,0:T(8,128)} %param.20) | copy-start | bytes 460804
  10.7 10.3 %copy-start.24 = (f32[768]{0:T(1024)S(1)}, f32[768]{0:T(1024)}, u32[]{:S(2)}) copy-start(f32[768]{0:T(1024)} %param.23) | copy-start | bytes 9220
  10.7 10.3 %copy-start.32 = (f32[768]{0:T(1024)S(1)}, f32[768]{0:T(1024)}, u32[]{:S(2)}) copy-start(f32[768]{0:T(1024)} %param.24) | copy-start | bytes 9220
  19.5 4.3 %copy-start.28 = (f32[768]{0:T(1024)S(1)}, f32[768]{0:T(1024)}, u32[]{:S(2)}) copy-start(f32[768]{0:T(1024)} %param.26) | copy-start | bytes 9220
  19.5 4.3 %copy-start.29 = (f32[768]{0:T(1024)S(1)}, f32[768]{0:T(1024)}, u32[]{:S(2)}) copy-start(f32[768]{0:T(1024)} %param.27) | copy-start | bytes 9220
  23.8 4.1 copy-start.3
  47.9 4.6 %copy-start.1 = (f32[4,12,248,248]{2,3,1,0:T(8,128)}, f32[4,12,248,248]{2,3,1,0:T(8,128)S(1)}, u32[]{:S(2)}) copy-start(f32[4,12,248,248]{2,3,1,0:T(8,128)S(1)} %get-tuple-element.39) | copy-start | bytes 35426308
  47.9 4.6 %copy-start.14 = (bf16[4,248,768]{1,2,0:T(8,128)(2,1)S(1)}, bf16[4,248,768]{1,2,0:T(8,128)(2,1)}, u32[]{:S(2)}) copy-start(bf16[4,248,768]{1,2,0:T(8,128)(2,1)} %copy.69) | copy-start | bytes 4571140
  52.5 3.2 copy-start.20
  52.5 3.2 copy-start.33
  57.5 43.4 %copy-start.4 = (f32[4,248,768]{2,1,0:T(8,128)}, f32[4,248,768]{2,1,0:T(8,128)S(1)}, u32[]{:S(2)}) copy-start(f32[4,248,768]{2,1,0:T(8,128)S(1)} %get-tuple-element.41) | copy-start | bytes 9142276
  71.9 29.0 %copy-start.35 = (f32[768]{0:T(1024)S(1)}, f32[768]{0:T(1024)}, u32[]{:S(2)}) copy-start(f32[768]{0:T(1024)} %param.35) | copy-start | bytes 9220
  100.9 14.7 %copy-start.18 = (bf16[4,198,768]{2,0,1:T(4,128)(2,1)S(1)}, bf16[4,198,768]{2,0,1:T(4,128)(2,1)}, u32[]{:S(2)}) copy-start(bf16[4,198,768]{2,0,1:T(4,128)(2,1)} %param.36) | copy-start | bytes 3649540
  137.5 3.7 copy-start.5
  137.5 4.6 %copy-start.10 = (f32[4,248,768]{2,1,0:T(8,128)S(1)}, f32[4,248,768]{2,1,0:T(8,128)}, u32[]{:S(2)}) copy-start(f32[4,248,768]{2,1,0:T(8,128)} %get-tuple-element.44) | copy-start | bytes 9142276
  151.5 14.4 %copy-start.7 = (bf16[4,248,768]{1,2,0:T(8,128)(2,1)S(1)}, bf16[4,248,768]{1,2,0:T(8,128)(2,1)}, u32[]{:S(2)}) copy-start(bf16[4,248,768]{1,2,0:T(8,128)(2,1)} %copy.76) | copy-start | bytes 4571140
  151.5 23.4 %slice-start = ((s8[12189696]{0:T(1024)(128)(4,1)}), s8[4194304]{0:T(1024)(128)(4,1)S(1)}, s32[]{:S(2)}) async-start(s8[12189696]{0:T(1024)(128)(4,1)} %bitcast.70), calls=%async_computation.2 | async-start | bytes 8388608
  151.5 23.4 %slice-start.1 = ((s8[12189696]{0:T(1024)(128)(4,1)}), s8[3801088]{0:T(1024)(128)(4,1)S(1)}, s32[]{:S(2)}) async-start(s8[12189696]{0:T(1024)(128)(4,1)} %bitcast.70), calls=%async_computation.3 | async-start | bytes 7602176
  165.8 9.0 %slice-start.2 = ((s8[12189696]{0:T(1024)(128)(4,1)}), s8[4194304]{0:T(1024)(128)(4,1)S(1)}, s32[]{:S(2)}) async-start(s8[12189696]{0:T(1024)(128)(4,1)} %bitcast.70), calls=%async_computation.4 | async-start | bytes 8388608
  174.8 7.0 %copy-start.6 = (bf16[4,248,768]{1,2,0:T(8,128)(2,1)S(1)}, bf16[4,248,768]{1,2,0:T(8,128)(2,1)}, u32[]{:S(2)}) copy-start(bf16[4,248,768]{1,2,0:T(8,128)(2,1)} %copy.70) | copy-start | bytes 4571140
  181.8 3.7 copy-start.2
  194.8 200.4 %all-gather.4.cloned.1.call-start = ((), (), s32[]{:S(2)}) async-start(), calls=%async_computation.1 | async-start | bytes 5677056 | tf_op jit(solution)/shard_map/all_gather | solution.py:214
  202.7 126.7 %copy-start.36 = (s32[4]{0:T(128)S(1)}, s32[4]{0:T(128)}, u32[]{:S(2)}) copy-start(s32[4]{0:T(128)} %param.22) | copy-start | bytes 52
  369.6 3.5 copy-start.16
  369.6 5.0 %slice-start.3 = ((bf16[4,248,768]{2,1,0:T(8,128)(2,1)}), bf16[4,50,768]{2,1,0:T(8,128)(2,1)S(1)}, s32[]{:S(2)}) async-start(bf16[4,248,768]{2,1,0:T(8,128)(2,1)} %copy-done.21), calls=%async_computation.5 | async-start | bytes 688128 | tf_op jit(solution)/shard_map/slice | solution.py:148
  377.9 3.5 copy-start.12
  377.9 3.9 copy-start.22
  381.8 3.3 copy-start.26
  381.8 4.3 %copy-start.19 = (bf16[4,198,768]{2,0,1:T(4,128)(2,1)S(1)}, bf16[4,198,768]{2,0,1:T(4,128)(2,1)}, u32[]{:S(2)}) copy-start(bf16[4,198,768]{2,0,1:T(4,128)(2,1)} %param.36) | copy-start | bytes 3649540
  (13 other events, 24.8 us)
Sparse Core Ops, SparseCore 0:
  194.9 128.5 all-reduce.2
  329.5 65.6 all-gather.3
